TPU v7x, 128 devices: a whole 4x4x4 slice. The times are simulated.
128 devices in a mesh: smp: 32 (over x, z, y_lo), col: 2 (over core), slab: 2 (over y_hi).
Axes of the slice: x: 4, y: 4 (y_hi: 2, y_lo: 2; y = y_hi * 2 + y_lo), z: 4, core: 2. Of those that a mesh axis runs over, the one named last changes fastest.
Arguments:
- jacobian: bfloat16 [1024, 32, 16384], P('smp', 'slab', 'col'), may hold values from -0.005722046 to 0.005722046
- local_energy: float32 [1024], P('smp'), may hold values from -6 to 6
Outputs:
- update: float32 [32, 16384], P('slab', ('col', 'smp'))
All inputs are finite; a program needn't handle non-finite values.
Results may differ from a plain program's by a relative error of at most 0.0085.
Values may be sent and summed in bfloat16 or wider, within the bound.
A program may use at most 192 MiB of HBM per device.

v0:
```python
import jax
import jax.numpy as jnp
from jax import lax
from jax.sharding import PartitionSpec as P

SLABS = 32
SLAB_COLS = 16384


def shards(jacobian, local_energy):
    energies = lax.all_gather(local_energy, "smp", axis=0, tiled=True)
    jacobian, energies = lax.optimization_barrier((jacobian, energies))
    samples = energies.shape[0]
    root_count = jnp.sqrt(jnp.float32(samples))
    eps = (energies - jnp.mean(energies)) / root_count
    columns = lax.all_to_all(jacobian, "smp", split_axis=2, concat_axis=0, tiled=True)
    slab_count = columns.shape[1]
    width = columns.shape[2]
    values = columns.astype(jnp.float32)
    mean_row = jnp.mean(values, axis=0, keepdims=True)
    centered = (
        ((values - mean_row) / root_count).astype(jnp.bfloat16).reshape(samples, slab_count * width)
    )
    partial_gram = jnp.dot(centered, centered.T, preferred_element_type=jnp.float32)
    gram = lax.psum(partial_gram, ("smp", "col", "slab"))
    shift = 0.01 * jnp.trace(gram) / samples
    factor = jnp.linalg.cholesky(gram + shift * jnp.eye(samples, dtype=jnp.float32))
    middle = lax.linalg.triangular_solve(factor, eps[:, None], left_side=True, lower=True)
    coeffs = lax.linalg.triangular_solve(
        factor, middle, left_side=True, lower=True, transpose_a=True
    )[:, 0]
    delta = jnp.dot(coeffs, centered.astype(jnp.float32), precision=lax.Precision.HIGHEST)
    squared = jnp.dot(
        coeffs,
        jnp.dot(gram, coeffs, precision=lax.Precision.HIGHEST),
        precision=lax.Precision.HIGHEST,
    )
    limit = 0.3 * jnp.sqrt(jnp.float32(SLABS * SLAB_COLS))
    scaled = -jnp.minimum(1.0, limit / jnp.sqrt(squared)) * delta
    return scaled.reshape(slab_count, width)


def solution(mesh):
    in_specs = (P("smp", "slab", "col"), P("smp"))
    out_specs = P("slab", ("col", "smp"))
    return jax.shard_map(shards, mesh=mesh, in_specs=in_specs, out_specs=out_specs, check_vma=False)
```

profile of v0, /device:TPU:1, one launch (start us, length us, event | category | flops | bytes accessed | tf_op | source)
XLA Modules:
  0.0 905.1 jit_solution(12480278940735346125)
XLA Ops:
  9.3 70.8 %all-reduce.1 = f32[1024]{0:T(1024)S(1)} all-reduce(f32[1024]{0:T(1024)S(1)} %dynamic-update-slice.47), channel_id=1, replica_groups=mesh['smp'=32,'col'=2,'slab'=2] {'smp'}, use_global_device_ids=true, to_apply=%add.1 | all-reduce | flops 1024 | bytes 8192 | tf_op jit(solution)/shard_map/optimization_barrier | solution.py:12
  80.1 45.6 %copy.65 = bf16[32,16,8192]{0,1,2:T(8,128)(2,1)} copy(bf16[32,16,8192]{2,1,0:T(8,128)(2,1)} %param.2) | data formatting | bytes 16777216 | tf_op jit(solution)/shard_map/optimization_barrier | solution.py:12
  125.7 39.8 %reshape.346 = bf16[32,2,65536]{2,1,0:T(2,128)(2,1)} reshape(bf16[8192,16,32]{2,1,0:T(8,128)(2,1)} %bitcast.343) | data formatting | bytes 16777216
  165.5 86.4 %all_to_all.4 = bf16[32,2,65536]{2,1,0:T(2,128)(2,1)} all-to-all(bf16[32,2,65536]{2,1,0:T(2,128)(2,1)} %reshape.346), channel_id=1, replica_groups=mesh['smp'=32,'col'=2,'slab'=2] {'smp'}, dimensions={0} | all-to-all | bytes 16777216 | tf_op jit(solution)/shard_map/all_to_all | solution.py:16
  251.9 30.6 %reshape.347 = bf16[8192,16,32]{2,1,0:T(8,128)(2,1)} reshape(bf16[32,2,65536]{2,1,0:T(2,128)(2,1)} %all_to_all.4) | data formatting | bytes 16777216
  282.5 44.0 %copy.66 = f32[32,16,32,256]{3,1,0,2:T(8,128)} copy(bf16[32,16,32,256]{0,1,3,2:T(8,128)(2,1)} %bitcast.342) | data formatting | bytes 25165824 | tf_op jit(solution)/shard_map/convert_element_type | solution.py:19
  326.6 6.9 bitcast_reduce_fusion
  333.5 7.2 fusion.1
  343.8 16.8 %fusion.5 = f32[1024,1024]{0,1:T(8,128)} fusion(bf16[1024,16,256]{2,1,0:T(8,128)(2,1)S(1)} %bitcast.345), kind=kOutput, calls=%fused_computation.15 | convolution fusion | flops 8589934592 | bytes 12582912 | tf_op jit(solution)/shard_map/dot_general | solution.py:24
  362.1 12.2 %copy.98 = bf16[128,8,16,256]{3,1,2,0:T(8,128)(2,1)} copy(bf16[128,8,16,256]{3,2,1,0:T(8,128)(2,1)} %bitcast.346) | data formatting | bytes 16777216
  374.3 155.4 %all-reduce.4.cloned.1.call-done = f32[1024,1024]{0,1:T(8,128)} async-done(((f32[1024,1024]{0,1:T(8,128)}), f32[1024,1024]{0,1:T(8,128)}) %all-reduce.4.cloned.1.call-update) | async-done | bytes 4194320 | tf_op jit(solution)/shard_map/psum | solution.py:25
  533.2 4.8 select_add_fusion
  538.0 5.7 copy.70
  550.2 11.7 %cholesky.222 = f32[128,128]{1,0:T(8,128)S(1)} custom-call(f32[128,128]{1,0:T(8,128)S(1)} %cholesky.577), custom_call_target="Cholesky" | custom-call | tf_op jit(solution)/shard_map/jit(cholesky)/cholesky | solution.py:27
  562.0 9.8 %custom-call.64 = f32[1,128,128]{1,2,0:T(8,128)S(1)} custom-call(f32[1,128,128]{2,1,0:T(8,128)S(1)} %get-tuple-element.56), custom_call_target="InvertDiagBlocksLowerTriangular" | custom-call | tf_op jit(solution)/shard_map/jit(cholesky)/cholesky | solution.py:27
  574.9 11.7 %cholesky.243 = f32[128,128]{1,0:T(8,128)S(1)} custom-call(f32[128,128]{1,0:T(8,128)S(1)} %cholesky.581), custom_call_target="Cholesky" | custom-call | tf_op jit(solution)/shard_map/jit(cholesky)/cholesky | solution.py:27
  589.7 9.8 %custom-call.65 = f32[1,128,128]{1,2,0:T(8,128)S(1)} custom-call(f32[1,128,128]{2,1,0:T(8,128)S(1)} %get-tuple-element.54), custom_call_target="InvertDiagBlocksLowerTriangular" | custom-call | tf_op jit(solution)/shard_map/jit(cholesky)/cholesky | solution.py:27
  605.1 11.7 %cholesky.466 = f32[128,128]{1,0:T(8,128)S(1)} custom-call(f32[128,128]{1,0:T(8,128)S(1)} %cholesky.586), custom_call_target="Cholesky" | custom-call | tf_op jit(solution)/shard_map/jit(cholesky)/cholesky | solution.py:27
  617.6 9.8 %custom-call.66 = f32[1,128,128]{1,2,0:T(8,128)S(1)} custom-call(f32[1,128,128]{2,1,0:T(8,128)S(1)} %get-tuple-element.52), custom_call_target="InvertDiagBlocksLowerTriangular" | custom-call | tf_op jit(solution)/shard_map/jit(cholesky)/cholesky | solution.py:27
  632.0 11.7 %cholesky.485 = f32[128,128]{1,0:T(8,128)S(1)} custom-call(f32[128,128]{1,0:T(8,128)S(1)} %cholesky.591), custom_call_target="Cholesky" | custom-call | tf_op jit(solution)/shard_map/jit(cholesky)/cholesky | solution.py:27
  644.5 9.8 %custom-call.67 = f32[1,128,128]{1,2,0:T(8,128)S(1)} custom-call(f32[1,128,128]{2,1,0:T(8,128)S(1)} %get-tuple-element.50), custom_call_target="InvertDiagBlocksLowerTriangular" | custom-call | tf_op jit(solution)/shard_map/jit(cholesky)/cholesky | solution.py:27
  658.6 12.1 %cholesky.504 = f32[128,128]{1,0:T(8,128)S(1)} custom-call(f32[128,128]{1,0:T(8,128)S(1)} %cholesky.596), custom_call_target="Cholesky" | custom-call | tf_op jit(solution)/shard_map/jit(cholesky)/cholesky | solution.py:27
  671.4 9.8 %custom-call.68 = f32[1,128,128]{1,2,0:T(8,128)S(1)} custom-call(f32[1,128,128]{2,1,0:T(8,128)S(1)} %get-tuple-element.48), custom_call_target="InvertDiagBlocksLowerTriangular" | custom-call | tf_op jit(solution)/shard_map/jit(cholesky)/cholesky | solution.py:27
  685.5 11.7 %cholesky.524 = f32[128,128]{1,0:T(8,128)S(1)} custom-call(f32[128,128]{1,0:T(8,128)S(1)} %cholesky.601), custom_call_target="Cholesky" | custom-call | tf_op jit(solution)/shard_map/jit(cholesky)/cholesky | solution.py:27
  698.0 9.8 %custom-call.69 = f32[1,128,128]{1,2,0:T(8,128)S(1)} custom-call(f32[1,128,128]{2,1,0:T(8,128)S(1)} %get-tuple-element.46), custom_call_target="InvertDiagBlocksLowerTriangular" | custom-call | tf_op jit(solution)/shard_map/jit(cholesky)/cholesky | solution.py:27
  711.6 11.7 %cholesky.544 = f32[128,128]{1,0:T(8,128)S(1)} custom-call(f32[128,128]{1,0:T(8,128)S(1)} %cholesky.606), custom_call_target="Cholesky" | custom-call | tf_op jit(solution)/shard_map/jit(cholesky)/cholesky | solution.py:27
  724.1 9.8 %custom-call.70 = f32[1,128,128]{1,2,0:T(8,128)S(1)} custom-call(f32[1,128,128]{2,1,0:T(8,128)S(1)} %get-tuple-element.44), custom_call_target="InvertDiagBlocksLowerTriangular" | custom-call | tf_op jit(solution)/shard_map/jit(cholesky)/cholesky | solution.py:27
  736.9 11.7 %cholesky.562 = f32[128,128]{1,0:T(8,128)S(1)} custom-call(f32[128,128]{1,0:T(8,128)S(1)} %convolution_subtract_fusion.6), custom_call_target="Cholesky" | custom-call | tf_op jit(solution)/shard_map/jit(cholesky)/cholesky | solution.py:27
  758.8 4.9 select_select_fusion
  763.7 24.5 %while.1 = (s32[]{:T(128)}, f32[1024,1024]{0,1:T(8,128)}, s32[8,2]{0,1:T(2,128)S(1)}, f32[8,128,128]{2,1,0:T(8,128)S(1)}, s32[]{:T(128)}) while((s32[]{:T(128)}, f32[1024,1024]{0,1:T(8,128)}, s32[8,2]{0,1:T(2,128)S(1)}, f32[8,128,128]{2,1,0:T(8,128)S(1)}, s32[]{:T(128)}) %tuple.54), condition=%wide.while_cond, body=%wide.while_body.sunk | while | flops 2 | bytes 393321 | solution.py:29
  788.2 78.8 %custom-call.71 = f32[8,128,128]{1,2,0:T(8,128)S(1)} custom-call(f32[8,128,128]{2,1,0:T(8,128)S(1)} %get-tuple-element.16), custom_call_target="InvertDiagBlocksLowerTriangular" | custom-call | tf_op jit(solution)/shard_map/triangular_solve | solution.py:29
  891.7 5.7 fusion.126
  (169 shorter events, 104.9 us)
Async XLA Ops:
  6.5 523.2 %all-reduce.4.cloned.1.call-start = ((), (), s32[]{:S(2)}) async-start(), calls=%async_computation.1 | async-start | bytes 8388608 | tf_op jit(solution)/shard_map/psum | solution.py:25
  340.6 3.2 copy-start.1
  548.3 2.0 copy-start.2
  867.0 21.1 %copy-start = (f32[1024,1024]{0,1:T(8,128)S(1)}, f32[1024,1024]{0,1:T(8,128)}, u32[]{:S(2)}) copy-start(f32[1024,1024]{0,1:T(8,128)} %all-reduce.4.cloned.1.call-done) | copy-start | bytes 12582916
Sparse Core Ops, SparseCore 0:
  360.8 168.8 all-reduce.3
where the time goes:
time: 912 us; the launch traced here: 905 us
  other arithmetic  279 us (31%)
  local copies, waits for them, and re-layouts  219 us (24%)
  blocking collectives  157 us (17%)
  waiting for transfers between devices  155 us (17%)
  matrix products  72.4 us (8%)
  between operations  21.5 us (2%)
    another operation x30, other arithmetic, shards(): jnp.linalg.cholesky(gram + shift * jnp.eye(samples, dtype=jnp.float32))  168 us
    psum x1, waiting for transfers between devices, shards(): gram = lax.psum(partial_gram, ('smp', 'col', 'slab'))  155 us
    unnamed x30, local copies, waits for them, and re-layouts  90.2 us
    all_to_all x1, blocking collectives, shards(): lax.all_to_all(jacobian, 'smp', split_axis=2, concat_axis=0, tiled=True)  86.4 us
    another operation x3, other arithmetic, shards(): lax.linalg.triangular_solve(factor, middle, left_side=True, lower=True, t...  83.7 us
    optimization_barrier x1, blocking collectives, shards(): jacobian, energies = lax.optimization_barrier((jacobian, energies))  70.8 us
    optimization_barrier x1, local copies, waits for them, and re-layouts, shards(): jacobian, energies = lax.optimization_barrier((jacobian, energies))  45.6 us
    convert_element_type x1, local copies, waits for them, and re-layouts, shards(): values = columns.astype(jnp.float32)  44 us
  transfers between devices with their start and end apart: 1, of which 1 were waited for; matrix products, arithmetic and copies ran while one was open for 1% of the time, Pallas kernels for 0%

commit v1 on v0

--- a/solution.py
+++ b/solution.py
@@ -22,7 +22,9 @@
         ((values - mean_row) / root_count).astype(jnp.bfloat16).reshape(samples, slab_count * width)
     )
     partial_gram = jnp.dot(centered, centered.T, preferred_element_type=jnp.float32)
-    gram = lax.psum(partial_gram, ("smp", "col", "slab"))
+    gram = partial_gram
+    for kk in (("col", "slab"), "smp"):
+        gram = lax.psum(gram, axis_name=kk)
     shift = 0.01 * jnp.trace(gram) / samples
     factor = jnp.linalg.cholesky(gram + shift * jnp.eye(samples, dtype=jnp.float32))
     middle = lax.linalg.triangular_solve(factor, eps[:, None], left_side=True, lower=True)

time: 912 us -> 1240 us (1.36)
  the two profiles are of different devices: /device:TPU:1 before, /device:TPU:16 now
where the time goes in v1:
time: 1240 us
  waiting for transfers between devices  473 us (38%)
  other arithmetic  279 us (22%)
  local copies, waits for them, and re-layouts  219 us (18%)
  blocking collectives  171 us (14%)
  matrix products  72.2 us (6%)
  between operations  21.6 us (2%)
    psum x2, waiting for transfers between devices, shards(): gram = lax.psum(gram, axis_name=kk)  473 us
    another operation x30, other arithmetic, shards(): jnp.linalg.cholesky(gram + shift * jnp.eye(samples, dtype=jnp.float32))  168 us
    unnamed x30, local copies, waits for them, and re-layouts  90.2 us
    all_to_all x1, blocking collectives, shards(): lax.all_to_all(jacobian, 'smp', split_axis=2, concat_axis=0, tiled=True)  87.4 us
    optimization_barrier x1, blocking collectives, shards(): jacobian, energies = lax.optimization_barrier((jacobian, energies))  83.8 us
    another operation x3, other arithmetic, shards(): lax.linalg.triangular_solve(factor, middle, left_side=True, lower=True, t...  83.7 us
    optimization_barrier x1, local copies, waits for them, and re-layouts, shards(): jacobian, energies = lax.optimization_barrier((jacobian, energies))  45.6 us
    convert_element_type x1, local copies, waits for them, and re-layouts, shards(): values = columns.astype(jnp.float32)  44 us
  transfers between devices with their start and end apart: 2, of which 2 were waited for; matrix products, arithmetic and copies ran while one was open for 1% of the time, Pallas kernels for 0%

profile of v1, /device:TPU:16, one launch (start us, length us, event | category | flops | bytes accessed | tf_op | source)
XLA Modules:
  0.0 1236.5 jit_solution(13328443616182696846)
XLA Ops:
  9.3 83.8 %all-reduce.1 = f32[1024]{0:T(1024)S(1)} all-reduce(f32[1024]{0:T(1024)S(1)} %dynamic-update-slice.47), channel_id=1, replica_groups=mesh['smp'=32,'col'=2,'slab'=2] {'smp'}, use_global_device_ids=true, to_apply=%add.1 | all-reduce | flops 1024 | bytes 8192 | tf_op jit(solution)/shard_map/optimization_barrier | solution.py:12
  93.1 45.6 %copy.65 = bf16[32,16,8192]{0,1,2:T(8,128)(2,1)} copy(bf16[32,16,8192]{2,1,0:T(8,128)(2,1)} %param.2) | data formatting | bytes 16777216 | tf_op jit(solution)/shard_map/optimization_barrier | solution.py:12
  138.6 39.8 %reshape.346 = bf16[32,2,65536]{2,1,0:T(2,128)(2,1)} reshape(bf16[8192,16,32]{2,1,0:T(8,128)(2,1)} %bitcast.343) | data formatting | bytes 16777216
  178.4 87.4 %all_to_all.4 = bf16[32,2,65536]{2,1,0:T(2,128)(2,1)} all-to-all(bf16[32,2,65536]{2,1,0:T(2,128)(2,1)} %reshape.346), channel_id=1, replica_groups=mesh['smp'=32,'col'=2,'slab'=2] {'smp'}, dimensions={0} | all-to-all | bytes 16777216 | tf_op jit(solution)/shard_map/all_to_all | solution.py:16
  265.8 30.6 %reshape.347 = bf16[8192,16,32]{2,1,0:T(8,128)(2,1)} reshape(bf16[32,2,65536]{2,1,0:T(2,128)(2,1)} %all_to_all.4) | data formatting | bytes 16777216
  296.4 44.0 %copy.66 = f32[32,16,32,256]{3,1,0,2:T(8,128)} copy(bf16[32,16,32,256]{0,1,3,2:T(8,128)(2,1)} %bitcast.342) | data formatting | bytes 25165824 | tf_op jit(solution)/shard_map/convert_element_type | solution.py:19
  340.5 6.9 bitcast_reduce_fusion
  347.4 7.2 fusion.1
  357.8 16.6 %fusion.5 = f32[1024,1024]{0,1:T(8,128)} fusion(bf16[1024,16,256]{2,1,0:T(8,128)(2,1)S(1)} %bitcast.345), kind=kOutput, calls=%fused_computation.15 | convolution fusion | flops 8589934592 | bytes 12582912 | tf_op jit(solution)/shard_map/dot_general | solution.py:24
  374.6 157.3 %all-reduce.5.cloned.1.call-done = f32[1024,1024]{0,1:T(8,128)} async-done(((f32[1024,1024]{0,1:T(8,128)}), f32[1024,1024]{0,1:T(8,128)}) %all-reduce.5.cloned.1.call-update) | async-done | bytes 4194320 | tf_op jit(solution)/shard_map/psum | solution.py:27
  533.3 12.2 copy.98
  545.6 315.6 %all-reduce.7.cloned.1.call-done = f32[1024,1024]{0,1:T(8,128)} async-done(((f32[1024,1024]{0,1:T(8,128)}), f32[1024,1024]{0,1:T(8,128)}) %all-reduce.7.cloned.1.call-update) | async-done | bytes 4194320 | tf_op jit(solution)/shard_map/psum | solution.py:27
  869.5 5.7 copy.70
  881.7 11.7 cholesky.222
  893.4 9.8 custom-call.64
  906.4 11.7 cholesky.243
  921.2 9.8 custom-call.65
  936.5 11.7 cholesky.466
  949.0 9.8 custom-call.66
  963.4 11.7 cholesky.485
  975.9 9.8 custom-call.67
  990.0 12.1 cholesky.504
  1002.9 9.8 custom-call.68
  1016.9 11.7 cholesky.524
  1029.4 9.8 custom-call.69
  1043.0 11.7 cholesky.544
  1055.5 9.8 custom-call.70
  1068.4 11.7 cholesky.562
  1090.3 4.9 select_select_fusion
  1095.1 24.5 %while.1 = (s32[]{:T(128)}, f32[1024,1024]{0,1:T(8,128)}, s32[8,2]{0,1:T(2,128)S(1)}, f32[8,128,128]{2,1,0:T(8,128)S(1)}, s32[]{:T(128)}) while((s32[]{:T(128)}, f32[1024,1024]{0,1:T(8,128)}, s32[8,2]{0,1:T(2,128)S(1)}, f32[8,128,128]{2,1,0:T(8,128)S(1)}, s32[]{:T(128)}) %tuple.54), condition=%wide.while_cond, body=%wide.while_body.sunk | while | flops 2 | bytes 393321 | solution.py:31
  1119.6 78.8 %custom-call.71 = f32[8,128,128]{1,2,0:T(8,128)S(1)} custom-call(f32[8,128,128]{2,1,0:T(8,128)S(1)} %get-tuple-element.16), custom_call_target="InvertDiagBlocksLowerTriangular" | custom-call | tf_op jit(solution)/shard_map/triangular_solve | solution.py:31
  1223.2 5.7 fusion.126
  (172 shorter events, 110.0 us)
Async XLA Ops:
  6.5 525.4 %all-reduce.5.cloned.1.call-start = ((), (), s32[]{:S(2)}) async-start(), calls=%async_computation.1 | async-start | bytes 8388608 | tf_op jit(solution)/shard_map/psum | solution.py:27
  354.5 3.2 copy-start.1
  374.3 486.8 %all-reduce.7.cloned.1.call-start = ((), (), s32[]{:S(2)}) async-start(), calls=%async_computation.2 | async-start | bytes 8388608 | tf_op jit(solution)/shard_map/psum | solution.py:27
  879.7 2.0 copy-start.2
  1198.4 21.1 %copy-start = (f32[1024,1024]{0,1:T(8,128)S(1)}, f32[1024,1024]{0,1:T(8,128)}, u32[]{:S(2)}) copy-start(f32[1024,1024]{0,1:T(8,128)} %all-reduce.7.cloned.1.call-done) | copy-start | bytes 12582916
Sparse Core Ops, SparseCore 0:
  374.5 157.3 all-reduce.4
  534.5 326.5 all-reduce.6
